TPU v7x, 32 devices: a whole 2x2x4 slice. The times are simulated.
32 devices in a mesh: row: 2 (over x), col: 16 (over z, y, core).
Axes of the slice: x: 2, y: 2, z: 4, core: 2. Of those that a mesh axis runs over, the one named last changes fastest.
Arguments:
- hessian_old: float32 [2048, 12288], P('row', 'col'), may hold values from -6 to 6
- gate_rows: bfloat16 [512, 2048], P('col', 'row'), may hold values from -9 to 9
- up_rows: bfloat16 [512, 2048], P('col', 'row'), may hold values from -15 to 15
- gate_columns: bfloat16 [512, 12288], P('row', 'col'), may hold values from -9 to 9
- up_columns: bfloat16 [512, 12288], P('row', 'col'), may hold values from -15 to 15
Outputs:
- hessian_new: float32 [2048, 12288], P('row', 'col')
All inputs are finite; a program needn't handle non-finite values.
Results may differ from a plain program's by a relative error of at most 0.00099.
Values may be sent and summed in bfloat16 or wider, within the bound.
A program may use at most 64 MiB of HBM per device.

v0:
```python
import jax
import jax.numpy as jnp
from jax import lax
from jax.sharding import PartitionSpec as P


def silu_product(gate, up):
    return (jax.nn.silu(gate.astype(jnp.float32)) * up.astype(jnp.float32)).astype(jnp.bfloat16)


def body(hessian_old, gate_rows, up_rows, gate_columns, up_columns):
    total_tokens = lax.axis_size("col") * gate_rows.shape[0]
    row_formed = silu_product(gate_rows, up_rows)
    column_formed = silu_product(gate_columns, up_columns)
    column_gathered = lax.all_gather(column_formed, "row", axis=0, tiled=True)
    product = lax.dot_general(
        lax.all_gather(row_formed, "col", axis=0, tiled=True),
        column_gathered,
        (((0,), (0,)), ((), ())),
        preferred_element_type=jnp.float32,
    )
    return 0.5 * hessian_old + product / total_tokens


def solution(mesh):
    in_specs = (P("row", "col"), P("col", "row"), P("col", "row"), P("row", "col"), P("row", "col"))
    out_specs = P("row", "col")
    return jax.shard_map(body, mesh=mesh, in_specs=in_specs, out_specs=out_specs, check_vma=False)
```

profile of v0, /device:TPU:1, one launch (start us, length us, event | category | flops | bytes accessed | tf_op | source)
XLA Modules:
  0.0 61.6 jit_solution(4926446980811626307)
XLA Ops:
  6.5 0.0 all-gather.2.cloned.1.call-start
  6.5 1.5 %fusion.9 = bf16[32,1024]{1,0:T(8,128)(2,1)} fusion(bf16[32,1024]{1,0:T(8,128)(2,1)} %param.7, bf16[32,1024]{1,0:T(8,128)(2,1)} %param.6), kind=kLoop, calls=%fused_computation.14 | loop fusion | flops 262144 | bytes 196608 | tf_op jit(solution)/shard_map/convert_element_type | solution.py:8
  8.1 0.0 all-gather.2.cloned.1.call-update
  8.1 1.4 %fusion.4 = bf16[256,768]{1,0:T(8,128)(2,1)S(1)} fusion(bf16[256,768]{1,0:T(8,128)(2,1)} %param.9, bf16[256,768]{1,0:T(8,128)(2,1)} %param.8), kind=kLoop, calls=%fused_computation.7 | loop fusion | flops 1572864 | bytes 1179648 | tf_op jit(solution)/shard_map/convert_element_type | solution.py:8
  9.5 11.5 %all_gather.7 = bf16[512,768]{1,0:T(8,128)(2,1)S(1)} all-gather(bf16[256,768]{1,0:T(8,128)(2,1)S(1)} %fusion.4), channel_id=1, replica_groups=mesh['row'=2,'col'=16] {'row'}, dimensions={0}, use_global_device_ids=true | all-gather | bytes 1179648 | tf_op jit(solution)/shard_map/all_gather | solution.py:15
  21.0 28.8 %all-gather.2.cloned.1.call-done = bf16[512,1024]{1,0:T(8,128)(2,1)} async-done(((bf16[32,1024]{1,0:T(8,128)(2,1)}), bf16[512,1024]{1,0:T(8,128)(2,1)}) %all-gather.2.cloned.1.call-update) | async-done | bytes 1048592 | tf_op jit(solution)/shard_map/all_gather | solution.py:17
  49.8 4.9 %multiply_add_fusion = f32[1024,768]{1,0:T(8,128)} fusion(f32[1024,768]{1,0:T(8,128)} %param.5, bf16[512,1024]{1,0:T(8,128)(2,1)} %all-gather.2.cloned.1.call-done, bf16[512,768]{1,0:T(8,128)(2,1)S(1)} %all_gather.7), kind=kOutput, calls=%fused_computation | convolution fusion | flops 807665664 | bytes 8126464 | tf_op jit(solution)/shard_map/dot_general | solution.py:16
Async XLA Ops:
  6.5 43.3 %all-gather.2.cloned.1.call-start = ((), (), s32[]{:S(2)}) async-start(), calls=%async_computation | async-start | bytes 1114112 | tf_op jit(solution)/shard_map/all_gather | solution.py:17
Sparse Core Ops, SparseCore 0:
  9.5 40.3 all-gather.1
where the time goes:
time: 62.1 us; the launch traced here: 61.6 us
  waiting for transfers between devices  28.9 us (47%)
  between operations  13.4 us (22%)
  blocking collectives  11.5 us (19%)
  matrix products  4.9 us (8%)
  other arithmetic  2.92 us (5%)
    all_gather x1, waiting for transfers between devices, body(): lax.all_gather(row_formed, 'col', axis=0, tiled=True)  28.8 us
    all_gather x1, blocking collectives, body(): column_gathered = lax.all_gather(column_formed, 'row', axis=0, tiled=True)  11.5 us
    dot_general x1, matrix products, body(): lax.dot_general(lax.all_gather(row_formed, 'col', axis=0, tiled=True), co...  4.9 us
    convert_element_type x2, other arithmetic, silu_product(): (jax.nn.silu(gate.astype(jnp.float32)) * up.astype(jnp.float32)).astype(j...  2.92 us
  transfers between devices with their start and end apart: 1, of which 1 were waited for; matrix products, arithmetic and copies ran while one was open for 2% of the time, Pallas kernels for 0%

commit v1 on v0

v1 whole, which is shorter than its diff:
```python
import functools

import jax
import jax.numpy as jnp
from jax import lax
from jax.experimental import pallas as pl
from jax.experimental.pallas import tpu as pltpu
from jax.sharding import PartitionSpec as P

MESH = pl.DeviceIdType.MESH


def silu_product(gate, up):
    return (jax.nn.silu(gate.astype(jnp.float32)) * up.astype(jnp.float32)).astype(jnp.bfloat16)


def partner(z, d, size):
    if size & (size - 1):
        return lax.rem(z + d, size), lax.rem(z + size - d, size)
    out, bit = z, 1
    while bit < size:
        if d & bit:
            out = out + bit * (1 - 2 * lax.rem(z // bit, 2))
        bit *= 2
    return out, out


def kernel(dims, old_hbm, gr_hbm, ur_hbm, gc_hbm, uc_hbm, out_ref, old, gr, ur, gc, uc, rows, cols, in_sem, old_sem, z_sem, y_sem, k_sem, x_sem, row_recv, col_recv):
    n_row, n_z, n_y, n_k, tiles, width, block = dims
    n_col = n_z * n_y * n_k
    depth = gc.shape[1]
    height = out_ref.shape[0]
    tokens = n_col * gr.shape[0]
    r = lax.axis_index("row")
    c = lax.axis_index("col")
    k = lax.rem(c, n_k)
    y = lax.rem(c // n_k, n_y)
    z = c // (n_k * n_y)

    def at(z_, y_, k_):
        return (z_ * n_y + y_) * n_k + k_

    z_to = [partner(z, d, n_z)[0] for d in range(n_z - 1, 0, -1)]
    z_from = [partner(z, d, n_z)[1] for d in range(n_z - 1, 0, -1)]
    other_y = [lax.rem(y + 1, n_y)] if n_y > 1 else []
    other_k = [lax.rem(k + 1, n_k)] if n_k > 1 else []
    r_to = [lax.rem(r + d, n_row) for d in range(1, n_row)]
    r_from = [lax.rem(r + n_row - d, n_row) for d in range(1, n_row)]

    barrier = pltpu.get_barrier_semaphore()
    peers = [{"col": at(t, y, k)} for t in z_to] + [{"col": at(z, t, k)} for t in other_y] + [{"col": at(z, y, t)} for t in other_k]
    peers += [{"row": t} for t in r_to]
    for peer in peers:
        pl.semaphore_signal(barrier, inc=1, device_id=peer, device_id_type=MESH)

    loads = [pltpu.make_async_copy(gr_hbm, gr, in_sem.at[0]), pltpu.make_async_copy(ur_hbm, ur, in_sem.at[1])]
    for j in range(tiles):
        part = pl.ds(j * width, width)
        loads.append(pltpu.make_async_copy(gc_hbm.at[:, part], gc.at[j], in_sem.at[2 + 2 * j]))
        loads.append(pltpu.make_async_copy(uc_hbm.at[:, part], uc.at[j], in_sem.at[3 + 2 * j]))
    for load in loads:
        load.start()
    old_load = pltpu.make_async_copy(old_hbm, old, old_sem)
    old_load.start()

    started = []

    def send_row(piece, sem, device):
        copy = pltpu.make_async_remote_copy(
            src_ref=rows.at[piece], dst_ref=rows.at[piece], send_sem=sem, recv_sem=row_recv.at[piece],
            device_id={"col": device}, device_id_type=MESH)
        copy.start()
        started.append(copy)

    def wait_row(piece):
        pltpu.make_async_remote_copy(
            src_ref=rows.at[piece], dst_ref=rows.at[piece], send_sem=k_sem.at[0], recv_sem=row_recv.at[piece],
            device_id={"col": c}, device_id_type=MESH).wait_recv()

    loads[0].wait()
    loads[1].wait()
    rows[c] = silu_product(gr[...], ur[...])
    loads[2].wait()
    loads[3].wait()
    cols[r, 0] = silu_product(gc[0], uc[0])
    pl.semaphore_wait(barrier, len(peers))

    for i, t in enumerate(z_to):
        send_row(c, z_sem.at[i], at(t, y, k))
    for t in other_y:
        send_row(c, y_sem.at[0], at(z, t, k))
    for t in other_k:
        send_row(c, k_sem.at[0], at(z, y, t))
    for j in range(tiles):
        if j:
            loads[2 + 2 * j].wait()
            loads[3 + 2 * j].wait()
            cols[r, j] = silu_product(gc[j], uc[j])
        for i, t in enumerate(r_to):
            copy = pltpu.make_async_remote_copy(
                src_ref=cols.at[r, j], dst_ref=cols.at[r, j], send_sem=x_sem.at[i, j], recv_sem=col_recv.at[r, j],
                device_id={"row": t}, device_id_type=MESH)
            copy.start()
            started.append(copy)

    used = 1

    def pass_on(piece):
        nonlocal used
        for t in other_k:
            send_row(piece, k_sem.at[used], at(z, y, t))
        used += 1

    for t in other_y:
        wait_row(at(z, t, k))
        pass_on(at(z, t, k))
    for i, s in enumerate(z_from):
        wait_row(at(s, y, k))
        for t in other_y:
            send_row(at(s, y, k), y_sem.at[1 + i], at(z, t, k))
        pass_on(at(s, y, k))
    for s in z_from:
        for t in other_y:
            wait_row(at(s, t, k))
            pass_on(at(s, t, k))
    for t in other_k:
        wait_row(at(z, y, t))
        for u in other_y:
            wait_row(at(z, u, t))
        for s in z_from:
            wait_row(at(s, y, t))
        for s in z_from:
            for u in other_y:
                wait_row(at(s, u, t))
    for s in r_from:
        for j in range(tiles):
            pltpu.make_async_remote_copy(
                src_ref=cols.at[s, j], dst_ref=cols.at[s, j], send_sem=x_sem.at[0, 0], recv_sem=col_recv.at[s, j],
                device_id={"row": r}, device_id_type=MESH).wait_recv()
    old_load.wait()

    share = n_col // n_row

    @pl.loop(0, height // block)
    def _(m):
        here = pl.ds(pl.multiple_of(m * block, block), block)
        for j in range(tiles):
            there = pl.ds(j * width, width)
            total = None
            for s in range(n_row):
                left = rows[pl.ds(s * share, share), :, here].reshape(depth, block)
                term = lax.dot_general(left, cols[s, j], (((0,), (0,)), ((), ())), preferred_element_type=jnp.float32)
                total = term if total is None else total + term
            total = total * (1.0 / tokens) if tokens & (tokens - 1) == 0 else total / tokens
            out_ref[here, there] = 0.5 * old[here, there] + total

    for copy in started:
        copy.wait_send()


def body(n_row, n_col, hessian_old, gate_rows, up_rows, gate_columns, up_columns):
    n_k = 2 if n_col % 2 == 0 else 1
    n_y = 2 if (n_col // n_k) % 2 == 0 else 1
    n_z = n_col // (n_k * n_y)
    height, span = hessian_old.shape
    piece = gate_rows.shape[0]
    depth = gate_columns.shape[0]
    width = 256 if span % 256 == 0 else span
    block = 256 if height % 256 == 0 else height
    tiles = span // width
    hbm_spec = pl.BlockSpec(memory_space=pltpu.HBM)
    return pl.pallas_call(
        functools.partial(kernel, (n_row, n_z, n_y, n_k, tiles, width, block)),
        out_shape=jax.ShapeDtypeStruct(hessian_old.shape, jnp.float32),
        in_specs=[hbm_spec] * 5,
        out_specs=pl.BlockSpec(memory_space=pltpu.VMEM),
        scratch_shapes=[
            pltpu.VMEM((height, span), jnp.float32),
            pltpu.VMEM((piece, height), jnp.bfloat16),
            pltpu.VMEM((piece, height), jnp.bfloat16),
            pltpu.VMEM((tiles, depth, width), jnp.bfloat16),
            pltpu.VMEM((tiles, depth, width), jnp.bfloat16),
            pltpu.VMEM((n_col, piece, height), jnp.bfloat16),
            pltpu.VMEM((n_row, tiles, depth, width), jnp.bfloat16),
            pltpu.SemaphoreType.DMA((2 + 2 * tiles,)),
            pltpu.SemaphoreType.DMA,
            pltpu.SemaphoreType.DMA((max(n_z - 1, 1),)),
            pltpu.SemaphoreType.DMA((n_z,)),
            pltpu.SemaphoreType.DMA((n_z * n_y,)),
            pltpu.SemaphoreType.DMA((max(n_row - 1, 1), tiles)),
            pltpu.SemaphoreType.DMA((n_col,)),
            pltpu.SemaphoreType.DMA((n_row, tiles)),
        ],
        compiler_params=pltpu.CompilerParams(collective_id=0, has_side_effects=True, vmem_limit_bytes=40 * 1024 * 1024),
        name="update",
    )(hessian_old, gate_rows, up_rows, gate_columns, up_columns)


def solution(mesh):
    in_specs = (P("row", "col"), P("col", "row"), P("col", "row"), P("row", "col"), P("row", "col"))
    out_specs = P("row", "col")
    step = functools.partial(body, mesh.shape["row"], mesh.shape["col"])
    return jax.shard_map(step, mesh=mesh, in_specs=in_specs, out_specs=out_specs, check_vma=False)
```

time: 62.1 us -> 26.7 us (0.43)
  waiting for transfers between devices: 28.9 us -> 0 us
  Pallas kernels: 0 us -> 19.1 us
  between operations: 13.4 us -> 0.01 us
  blocking collectives: 11.5 us -> 0 us
  local copies, waits for them, and re-layouts: 0 us -> 7.22 us
  matrix products: 4.9 us -> 0 us
  other arithmetic: 2.92 us -> 0 us
    all_gather x1 -> x0, waiting for transfers between devices: 28.8 us -> none  [body(): lax.all_gather(row_formed, 'col', axis=0, tiled=True)]
    pallas_call x0 -> x1, Pallas kernels: none -> 19.1 us  [body(): pl.pallas_call(functools.partial(kernel, (n_row, n_z, n_y, n_k, tiles, wi...]
    all_gather x1 -> x0, blocking collectives: 11.5 us -> none  [body(): column_gathered = lax.all_gather(column_formed, 'row', axis=0, tiled=True)]
    unnamed x0 -> x11, local copies, waits for them, and re-layouts: none -> 7.22 us
    dot_general x1 -> x0, matrix products: 4.9 us -> none  [body(): lax.dot_general(lax.all_gather(row_formed, 'col', axis=0, tiled=True), co...]
    convert_element_type x2 -> x0, other arithmetic: 2.92 us -> none  [silu_product(): (jax.nn.silu(gate.astype(jnp.float32)) * up.astype(jnp.float32)).astype(j...]
  transfers between devices with their start and end apart: 1 -> 0, of which waited for: 1 -> 0; matrix products, arithmetic and copies ran while one was open for 2% -> 0% of each run, Pallas kernels for 0% -> 0%
where the time goes in v1:
time: 26.7 us; the launch traced here: 26.4 us
  Pallas kernels  19.1 us (72%)
  local copies, waits for them, and re-layouts  7.22 us (27%)
    pallas_call x1, Pallas kernels, body(): pl.pallas_call(functools.partial(kernel, (n_row, n_z, n_y, n_k, tiles, wi...  19.1 us
    unnamed x11, local copies, waits for them, and re-layouts  7.22 us

profile of v1, /device:TPU:1, one launch (start us, length us, event | category | flops | bytes accessed | tf_op | source)
XLA Modules:
  0.0 26.4 jit_solution(13578882698740535506)
XLA Ops:
  0.0 0.0 copy-start
  0.0 1.9 %copy-done = f32[1024,768]{1,0:T(8,128)S(1)} copy-done((f32[1024,768]{1,0:T(8,128)S(1)}, f32[1024,768]{1,0:T(8,128)}, u32[]{:S(2)}) %copy-start) | copy-done | bytes 3145752
  1.9 0.0 copy-start.1
  1.9 1.0 %copy-done.1 = bf16[256,768]{1,0:T(8,128)(2,1)S(1)} copy-done((bf16[256,768]{1,0:T(8,128)(2,1)S(1)}, bf16[256,768]{1,0:T(8,128)(2,1)}, u32[]{:S(2)}) %copy-start.1) | copy-done | bytes 393240
  2.9 0.0 copy-start.2
  2.9 1.0 %copy-done.2 = bf16[256,768]{1,0:T(8,128)(2,1)S(1)} copy-done((bf16[256,768]{1,0:T(8,128)(2,1)S(1)}, bf16[256,768]{1,0:T(8,128)(2,1)}, u32[]{:S(2)}) %copy-start.2) | copy-done | bytes 393240
  3.9 0.0 copy-start.3
  3.9 0.8 %copy-done.3 = bf16[32,1024]{1,0:T(8,128)(2,1)S(1)} copy-done((bf16[32,1024]{1,0:T(8,128)(2,1)S(1)}, bf16[32,1024]{1,0:T(8,128)(2,1)}, u32[]{:S(2)}) %copy-start.3) | copy-done | bytes 65560
  4.7 0.0 copy-start.4
  4.7 0.8 %copy-done.4 = bf16[32,1024]{1,0:T(8,128)(2,1)S(1)} copy-done((bf16[32,1024]{1,0:T(8,128)(2,1)S(1)}, bf16[32,1024]{1,0:T(8,128)(2,1)}, u32[]{:S(2)}) %copy-start.4) | copy-done | bytes 65560
  5.6 19.1 %update.1 = f32[1024,768]{1,0:T(8,128)S(1)} custom-call(f32[1024,768]{1,0:T(8,128)S(1)} %copy-done, bf16[32,1024]{1,0:T(8,128)(2,1)S(1)} %copy-done.3, bf16[32,1024]{1,0:T(8,128)(2,1)S(1)} %copy-done.4, bf16[256,768]{1,0:T(8,128)(2,1)S(1)} %copy-done.1, bf16[256,768]{1,0:T(8,128)(2,1)S(1)} %copy-done.2), custom_call_target="tpu_custom_call" | custom-call | tf_op jit(solution)/shard_map/update/pallas_call | solution.py:172
  24.7 1.7 %copy.7 = f32[1024,768]{1,0:T(8,128)} copy(f32[1024,768]{1,0:T(8,128)S(1)} %update.1) | data formatting | bytes 6291456
Async XLA Ops:
  0.0 1.9 %copy-start = (f32[1024,768]{1,0:T(8,128)S(1)}, f32[1024,768]{1,0:T(8,128)}, u32[]{:S(2)}) copy-start(f32[1024,768]{1,0:T(8,128)} %old_hbm.1) | copy-start | bytes 9437188
  1.9 1.0 %copy-start.1 = (bf16[256,768]{1,0:T(8,128)(2,1)S(1)}, bf16[256,768]{1,0:T(8,128)(2,1)}, u32[]{:S(2)}) copy-start(bf16[256,768]{1,0:T(8,128)(2,1)} %gc_hbm.1) | copy-start | bytes 1179652
  2.9 1.0 %copy-start.2 = (bf16[256,768]{1,0:T(8,128)(2,1)S(1)}, bf16[256,768]{1,0:T(8,128)(2,1)}, u32[]{:S(2)}) copy-start(bf16[256,768]{1,0:T(8,128)(2,1)} %uc_hbm.1) | copy-start | bytes 1179652
  3.9 0.8 %copy-start.3 = (bf16[32,1024]{1,0:T(8,128)(2,1)S(1)}, bf16[32,1024]{1,0:T(8,128)(2,1)}, u32[]{:S(2)}) copy-start(bf16[32,1024]{1,0:T(8,128)(2,1)} %gr_hbm.1) | copy-start | bytes 196612
  4.7 0.8 %copy-start.4 = (bf16[32,1024]{1,0:T(8,128)(2,1)S(1)}, bf16[32,1024]{1,0:T(8,128)(2,1)}, u32[]{:S(2)}) copy-start(bf16[32,1024]{1,0:T(8,128)(2,1)} %ur_hbm.1) | copy-start | bytes 196612

commit v2 on v1

--- a/solution.py
+++ b/solution.py
@@ -25,12 +25,9 @@
     return out, out
 
 
-def kernel(dims, old_hbm, gr_hbm, ur_hbm, gc_hbm, uc_hbm, out_ref, old, gr, ur, gc, uc, rows, cols, in_sem, old_sem, z_sem, y_sem, k_sem, x_sem, row_recv, col_recv):
-    n_row, n_z, n_y, n_k, tiles, width, block = dims
+def gather_kernel(dims, old_hbm, gr_hbm, ur_hbm, gc_hbm, uc_hbm, old, rows, cols, gr, ur, gc, uc, in_sem, old_sem, z_sem, y_sem, k_sem, x_sem, row_recv, col_recv):
+    n_row, n_z, n_y, n_k, tiles, width = dims
     n_col = n_z * n_y * n_k
-    depth = gc.shape[1]
-    height = out_ref.shape[0]
-    tokens = n_col * gr.shape[0]
     r = lax.axis_index("row")
     c = lax.axis_index("col")
     k = lax.rem(c, n_k)
@@ -40,8 +37,8 @@
     def at(z_, y_, k_):
         return (z_ * n_y + y_) * n_k + k_
 
-    z_to = [partner(z, d, n_z)[0] for d in range(n_z - 1, 0, -1)]
-    z_from = [partner(z, d, n_z)[1] for d in range(n_z - 1, 0, -1)]
+    z_to = [partner(z, d, n_z)[0] for d in range(1, n_z)]
+    z_from = [partner(z, d, n_z)[1] for d in range(1, n_z)]
     other_y = [lax.rem(y + 1, n_y)] if n_y > 1 else []
     other_k = [lax.rem(k + 1, n_k)] if n_k > 1 else []
     r_to = [lax.rem(r + d, n_row) for d in range(1, n_row)]
@@ -139,11 +136,18 @@
                 device_id={"row": r}, device_id_type=MESH).wait_recv()
     old_load.wait()
 
+    for copy in started:
+        copy.wait_send()
+
+
+def product_kernel(block, old, rows, cols, out_hbm, out, sem):
+    n_col, piece, height = rows.shape
+    n_row, tiles, depth, width = cols.shape
+    tokens = n_col * piece
     share = n_col // n_row
-
-    @pl.loop(0, height // block)
-    def _(m):
-        here = pl.ds(pl.multiple_of(m * block, block), block)
+    stores = []
+    for m in range(height // block):
+        here = pl.ds(m * block, block)
         for j in range(tiles):
             there = pl.ds(j * width, width)
             total = None
@@ -152,10 +156,12 @@
                 term = lax.dot_general(left, cols[s, j], (((0,), (0,)), ((), ())), preferred_element_type=jnp.float32)
                 total = term if total is None else total + term
             total = total * (1.0 / tokens) if tokens & (tokens - 1) == 0 else total / tokens
-            out_ref[here, there] = 0.5 * old[here, there] + total
-
-    for copy in started:
-        copy.wait_send()
+            out[here, there] = 0.5 * old[here, there] + total
+        store = pltpu.make_async_copy(out.at[here], out_hbm.at[here], sem.at[m])
+        store.start()
+        stores.append(store)
+    for store in stores:
+        store.wait()
 
 
 def body(n_row, n_col, hessian_old, gate_rows, up_rows, gate_columns, up_columns):
@@ -166,22 +172,25 @@
     piece = gate_rows.shape[0]
     depth = gate_columns.shape[0]
     width = 256 if span % 256 == 0 else span
-    block = 256 if height % 256 == 0 else height
+    block = 128 if height % 128 == 0 else height
     tiles = span // width
-    hbm_spec = pl.BlockSpec(memory_space=pltpu.HBM)
-    return pl.pallas_call(
-        functools.partial(kernel, (n_row, n_z, n_y, n_k, tiles, width, block)),
-        out_shape=jax.ShapeDtypeStruct(hessian_old.shape, jnp.float32),
-        in_specs=[hbm_spec] * 5,
-        out_specs=pl.BlockSpec(memory_space=pltpu.VMEM),
+    inputs = (hessian_old, gate_rows, up_rows, gate_columns, up_columns)
+    vmem = pl.BlockSpec(memory_space=pltpu.VMEM)
+    hbm = pl.BlockSpec(memory_space=pltpu.HBM)
+    gathered = pl.pallas_call(
+        functools.partial(gather_kernel, (n_row, n_z, n_y, n_k, tiles, width)),
+        out_shape=(
+            pltpu.VMEM((height, span), jnp.float32),
+            pltpu.VMEM((n_col, piece, height), jnp.bfloat16),
+            pltpu.VMEM((n_row, tiles, depth, width), jnp.bfloat16),
+        ),
+        in_specs=[hbm] * len(inputs),
+        out_specs=(vmem, vmem, vmem),
         scratch_shapes=[
-            pltpu.VMEM((height, span), jnp.float32),
             pltpu.VMEM((piece, height), jnp.bfloat16),
             pltpu.VMEM((piece, height), jnp.bfloat16),
             pltpu.VMEM((tiles, depth, width), jnp.bfloat16),
             pltpu.VMEM((tiles, depth, width), jnp.bfloat16),
-            pltpu.VMEM((n_col, piece, height), jnp.bfloat16),
-            pltpu.VMEM((n_row, tiles, depth, width), jnp.bfloat16),
             pltpu.SemaphoreType.DMA((2 + 2 * tiles,)),
             pltpu.SemaphoreType.DMA,
             pltpu.SemaphoreType.DMA((max(n_z - 1, 1),)),
@@ -191,9 +200,18 @@
             pltpu.SemaphoreType.DMA((n_col,)),
             pltpu.SemaphoreType.DMA((n_row, tiles)),
         ],
-        compiler_params=pltpu.CompilerParams(collective_id=0, has_side_effects=True, vmem_limit_bytes=40 * 1024 * 1024),
-        name="update",
-    )(hessian_old, gate_rows, up_rows, gate_columns, up_columns)
+        compiler_params=pltpu.CompilerParams(collective_id=0, has_side_effects=True, vmem_limit_bytes=24 * 1024 * 1024),
+        name="gather",
+    )(*(pltpu.with_memory_space_constraint(a, pltpu.HBM) for a in inputs))
+    return pl.pallas_call(
+        functools.partial(product_kernel, block),
+        out_shape=jax.ShapeDtypeStruct((height, span), jnp.float32),
+        in_specs=[vmem] * 3,
+        out_specs=hbm,
+        scratch_shapes=[pltpu.VMEM((height, span), jnp.float32), pltpu.SemaphoreType.DMA((height // block,))],
+        compiler_params=pltpu.CompilerParams(vmem_limit_bytes=24 * 1024 * 1024),
+        name="product",
+    )(*gathered)
 
 
 def solution(mesh):

time: 26.7 us -> 18.5 us (0.69)
  local copies, waits for them, and re-layouts: 7.22 us -> 0 us
  Pallas kernels: 19.1 us -> 18.3 us
    unnamed x11 -> x0, local copies, waits for them, and re-layouts: 7.22 us -> none
    pallas_call x1 -> x2, Pallas kernels: 19.1 us -> 18.3 us  [the longest x1 16.2 us: body(): pl.pallas_call(functools.partial(gather_kernel, (n_row, n_z, n_y, n_k, ti...]
where the time goes in v2:
time: 18.5 us; the launch traced here: 18.3 us
  Pallas kernels  18.3 us (99%)
    pallas_call x1, Pallas kernels, body(): pl.pallas_call(functools.partial(gather_kernel, (n_row, n_z, n_y, n_k, ti...  16.2 us
    pallas_call x1, Pallas kernels, body(): pl.pallas_call(functools.partial(product_kernel, block), out_shape=jax.Sh...  2.1 us

profile of v2, /device:TPU:1, one launch (start us, length us, event | category | flops | bytes accessed | tf_op | source)
XLA Modules:
  0.0 18.3 jit_solution(16269454283501024394)
XLA Ops:
  0.0 16.2 %gather.1 = (f32[1024,768]{1,0:T(8,128)S(1)}, bf16[16,32,1024]{2,1,0:T(8,128)(2,1)S(1)}, bf16[2,3,256,256]{3,2,1,0:T(8,128)(2,1)S(1)}) custom-call(f32[1024,768]{1,0:T(8,128)} %old_hbm.1, bf16[32,1024]{1,0:T(8,128)(2,1)} %gr_hbm.1, bf16[32,1024]{1,0:T(8,128)(2,1)} %ur_hbm.1, bf16[256,768]{1,0:T(8,128)(2,1)} %gc_hbm.1, bf16[256,768]{1,0:T(8,128)(2,1)} %uc_hbm.1), custom_call_target="tpu_custom_call" | custom-call | tf_op jit(solution)/shard_map/gather/pallas_call | solution.py:180
  16.2 2.1 %product.1 = f32[1024,768]{1,0:T(8,128)} custom-call(f32[1024,768]{1,0:T(8,128)S(1)} %get-tuple-element.8.old, bf16[16,32,1024]{2,1,0:T(8,128)(2,1)S(1)} %get-tuple-element.9.rows, bf16[2,3,256,256]{3,2,1,0:T(8,128)(2,1)S(1)} %get-tuple-element.10.cols), custom_call_target="tpu_custom_call" | custom-call | tf_op jit(solution)/shard_map/product/pallas_call | solution.py:206

commit v3 on v2

v3 whole, which is shorter than its diff:
```python
import functools

import jax
import jax.numpy as jnp
from jax import lax
from jax.experimental import pallas as pl
from jax.experimental.pallas import tpu as pltpu
from jax.sharding import PartitionSpec as P

MESH = pl.DeviceIdType.MESH


def silu_product(gate, up):
    return (jax.nn.silu(gate.astype(jnp.float32)) * up.astype(jnp.float32)).astype(jnp.bfloat16)


def partner(z, d, size):
    if size & (size - 1):
        return lax.rem(z + d, size), lax.rem(z + size - d, size)
    out, bit = z, 1
    while bit < size:
        if d & bit:
            out = out + bit * (1 - 2 * lax.rem(z // bit, 2))
        bit *= 2
    return out, out


def gather_kernel(dims, old_hbm, gr_hbm, ur_hbm, gc_hbm, uc_hbm, old, rows, cols, gr, ur, gc, uc, in_sem, old_sem, z_sem, y_sem, k_sem, x_sem, row_recv, col_recv):
    n_row, n_z, n_y, n_k, tiles, width, splits, cuts = dims
    n_col = n_z * n_y * n_k
    r = lax.axis_index("row")
    c = lax.axis_index("col")
    k = lax.rem(c, n_k)
    y = lax.rem(c // n_k, n_y)
    z = c // (n_k * n_y)

    def at(z_, y_, k_):
        return (z_ * n_y + y_) * n_k + k_

    z_to = [partner(z, d, n_z)[0] for d in range(1, n_z)]
    z_from = [partner(z, d, n_z)[1] for d in range(1, n_z)]
    other_y = [lax.rem(y + 1, n_y)] if n_y > 1 else []
    other_k = [lax.rem(k + 1, n_k)] if n_k > 1 else []
    r_to = [lax.rem(r + d, n_row) for d in range(1, n_row)]
    r_from = [lax.rem(r + n_row - d, n_row) for d in range(1, n_row)]

    barrier = pltpu.get_barrier_semaphore()
    peers = [{"col": at(t, y, k)} for t in z_to] + [{"col": at(z, t, k)} for t in other_y] + [{"col": at(z, y, t)} for t in other_k]
    peers += [{"row": t} for t in r_to]
    for peer in peers:
        pl.semaphore_signal(barrier, inc=1, device_id=peer, device_id_type=MESH)

    thick = gr.shape[0] // splits
    deep = gc.shape[1] // cuts
    chunks = [(j, pl.ds(q * deep, deep), j * cuts + q) for j in range(tiles) for q in range(cuts)]
    row_loads = [pltpu.make_async_copy(gr_hbm, gr, in_sem.at[0]), pltpu.make_async_copy(ur_hbm, ur, in_sem.at[1])]
    col_loads = []
    for j, part, n in chunks:
        across = pl.ds(j * width, width)
        col_loads.append((
            pltpu.make_async_copy(gc_hbm.at[part, across], gc.at[j, part], in_sem.at[2 + 2 * n]),
            pltpu.make_async_copy(uc_hbm.at[part, across], uc.at[j, part], in_sem.at[3 + 2 * n])))
    for load in row_loads:
        load.start()
    for pair in col_loads:
        for load in pair:
            load.start()
    old_load = pltpu.make_async_copy(old_hbm, old, old_sem)

    started = []

    def row_copy(piece, h, sem, device):
        part = rows.at[piece, pl.ds(h * thick, thick)]
        return pltpu.make_async_remote_copy(
            src_ref=part, dst_ref=part, send_sem=sem, recv_sem=row_recv.at[piece, h],
            device_id={"col": device}, device_id_type=MESH)

    def send_row(piece, h, sem, device):
        copy = row_copy(piece, h, sem, device)
        copy.start()
        started.append(copy)

    def wait_row(piece, h):
        row_copy(piece, h, k_sem.at[0, 0], c).wait_recv()

    def col_copy(s, chunk, sem, device):
        j, part, n = chunk
        part = cols.at[j, s, part]
        return pltpu.make_async_remote_copy(
            src_ref=part, dst_ref=part, send_sem=sem, recv_sem=col_recv.at[s, n],
            device_id={"row": device}, device_id_type=MESH)

    def form_cols(chunk):
        j, part, n = chunk
        for load in col_loads[n]:
            load.wait()
        cols[j, r, part] = silu_product(gc[j, part], uc[j, part])

    def send_cols(chunk):
        for i, t in enumerate(r_to):
            copy = col_copy(r, chunk, x_sem.at[i, chunk[2]], t)
            copy.start()
            started.append(copy)

    def send_own_rows():
        for h in range(splits):
            for t in other_y:
                send_row(c, h, y_sem.at[0, h], at(z, t, k))
            for t in other_k:
                send_row(c, h, k_sem.at[0, h], at(z, y, t))
        for i, t in enumerate(z_to):
            for h in range(splits):
                send_row(c, h, z_sem.at[i, h], at(t, y, k))

    for load in row_loads:
        load.wait()
    rows[c] = silu_product(gr[...], ur[...])
    pl.semaphore_wait(barrier, len(peers))
    send_own_rows()
    form_cols(chunks[0])
    send_cols(chunks[0])
    for chunk in chunks[1:]:
        form_cols(chunk)
        send_cols(chunk)
    old_load.start()

    used = 1
    for t in other_y:
        for h in range(splits):
            wait_row(at(z, t, k), h)
            for u in other_k:
                send_row(at(z, t, k), h, k_sem.at[used, h], at(z, y, u))
    used += len(other_y)
    for i, s in enumerate(z_from):
        for h in range(splits):
            wait_row(at(s, y, k), h)
            for t in other_y:
                send_row(at(s, y, k), h, y_sem.at[1 + i, h], at(z, t, k))
            for u in other_k:
                send_row(at(s, y, k), h, k_sem.at[used + i, h], at(z, y, u))
    used += len(z_from)
    for i, s in enumerate(z_from):
        for t in other_y:
            for h in range(splits):
                wait_row(at(s, t, k), h)
                for u in other_k:
                    send_row(at(s, t, k), h, k_sem.at[used + i, h], at(z, y, u))
    for t in other_k:
        for s in [z] + z_from:
            for u in [y] + other_y:
                for h in range(splits):
                    wait_row(at(s, u, t), h)
    for s in r_from:
        for chunk in chunks:
            col_copy(s, chunk, x_sem.at[0, 0], r).wait_recv()
    old_load.wait()

    for copy in started:
        copy.wait_send()


def product_kernel(block, old, rows, cols, out_hbm, out, sem):
    n_col, piece, height = rows.shape
    tiles, n_row, depth, width = cols.shape
    tokens = n_col * piece
    stores = []
    for m in range(height // block):
        here = pl.ds(m * block, block)
        left = rows[:, :, here].reshape(tokens, block)
        for j in range(tiles):
            there = pl.ds(j * width, width)
            right = cols[j].reshape(tokens, width)
            total = lax.dot_general(left, right, (((0,), (0,)), ((), ())), preferred_element_type=jnp.float32)
            total = total * (1.0 / tokens) if tokens & (tokens - 1) == 0 else total / tokens
            out[here, there] = 0.5 * old[here, there] + total
        store = pltpu.make_async_copy(out.at[here], out_hbm.at[here], sem.at[m])
        store.start()
        stores.append(store)
    for store in stores:
        store.wait()


def body(n_row, n_col, hessian_old, gate_rows, up_rows, gate_columns, up_columns):
    n_k = 2 if n_col % 2 == 0 else 1
    n_y = 2 if (n_col // n_k) % 2 == 0 else 1
    n_z = n_col // (n_k * n_y)
    height, span = hessian_old.shape
    piece = gate_rows.shape[0]
    depth = gate_columns.shape[0]
    width = 256 if span % 256 == 0 else span
    block = 128 if height % 128 == 0 else height
    tiles = span // width
    splits = 2 if piece % (16 * 2) == 0 else 1
    cuts = 1 if depth % (16 * 1) == 0 else 1
    inputs = (hessian_old, gate_rows, up_rows, gate_columns, up_columns)
    vmem = pl.BlockSpec(memory_space=pltpu.VMEM)
    hbm = pl.BlockSpec(memory_space=pltpu.HBM)
    gathered = pl.pallas_call(
        functools.partial(gather_kernel, (n_row, n_z, n_y, n_k, tiles, width, splits, cuts)),
        out_shape=(
            pltpu.VMEM((height, span), jnp.float32),
            pltpu.VMEM((n_col, piece, height), jnp.bfloat16),
            pltpu.VMEM((tiles, n_row, depth, width), jnp.bfloat16),
        ),
        in_specs=[hbm] * len(inputs),
        out_specs=(vmem, vmem, vmem),
        scratch_shapes=[
            pltpu.VMEM((piece, height), jnp.bfloat16),
            pltpu.VMEM((piece, height), jnp.bfloat16),
            pltpu.VMEM((tiles, depth, width), jnp.bfloat16),
            pltpu.VMEM((tiles, depth, width), jnp.bfloat16),
            pltpu.SemaphoreType.DMA((2 + 2 * tiles * cuts,)),
            pltpu.SemaphoreType.DMA,
            pltpu.SemaphoreType.DMA((max(n_z - 1, 1), splits)),
            pltpu.SemaphoreType.DMA((n_z, splits)),
            pltpu.SemaphoreType.DMA((n_z * n_y, splits)),
            pltpu.SemaphoreType.DMA((max(n_row - 1, 1), tiles * cuts)),
            pltpu.SemaphoreType.DMA((n_col, splits)),
            pltpu.SemaphoreType.DMA((n_row, tiles * cuts)),
        ],
        compiler_params=pltpu.CompilerParams(collective_id=0, has_side_effects=True, vmem_limit_bytes=24 * 1024 * 1024),
        name="gather",
    )(*(pltpu.with_memory_space_constraint(a, pltpu.HBM) for a in inputs))
    return pl.pallas_call(
        functools.partial(product_kernel, block),
        out_shape=jax.ShapeDtypeStruct((height, span), jnp.float32),
        in_specs=[vmem] * 3,
        out_specs=hbm,
        scratch_shapes=[pltpu.VMEM((height, span), jnp.float32), pltpu.SemaphoreType.DMA((height // block,))],
        compiler_params=pltpu.CompilerParams(vmem_limit_bytes=24 * 1024 * 1024),
        name="product",
    )(*gathered)


def solution(mesh):
    in_specs = (P("row", "col"), P("col", "row"), P("col", "row"), P("row", "col"), P("row", "col"))
    out_specs = P("row", "col")
    step = functools.partial(body, mesh.shape["row"], mesh.shape["col"])
    return jax.shard_map(step, mesh=mesh, in_specs=in_specs, out_specs=out_specs, check_vma=False)
```

time: 18.5 us -> 18.5 us (level)
  no operation moved by 1% of the time
where the time goes in v3:
time: 18.5 us; the launch traced here: 18.2 us
  Pallas kernels  18.2 us (98%)
    pallas_call x1, Pallas kernels, body(): pl.pallas_call(functools.partial(gather_kernel, (n_row, n_z, n_y, n_k, ti...  16.1 us
    pallas_call x1, Pallas kernels, body(): pl.pallas_call(functools.partial(product_kernel, block), out_shape=jax.Sh...  2.08 us

profile of v3, /device:TPU:1, one launch (start us, length us, event | category | flops | bytes accessed | tf_op | source)
XLA Modules:
  0.0 18.2 jit_solution(9201667288245953467)
XLA Ops:
  0.0 16.1 %gather.1 = (f32[1024,768]{1,0:T(8,128)S(1)}, bf16[16,32,1024]{2,1,0:T(8,128)(2,1)S(1)}, bf16[3,2,256,256]{3,2,1,0:T(8,128)(2,1)S(1)}) custom-call(f32[1024,768]{1,0:T(8,128)} %old_hbm.1, bf16[32,1024]{1,0:T(8,128)(2,1)} %gr_hbm.1, bf16[32,1024]{1,0:T(8,128)(2,1)} %ur_hbm.1, bf16[256,768]{1,0:T(8,128)(2,1)} %gc_hbm.1, bf16[256,768]{1,0:T(8,128)(2,1)} %uc_hbm.1), custom_call_target="tpu_custom_call" | custom-call | tf_op jit(solution)/shard_map/gather/pallas_call | solution.py:198
  16.1 2.1 %product.1 = f32[1024,768]{1,0:T(8,128)} custom-call(f32[1024,768]{1,0:T(8,128)S(1)} %get-tuple-element.8.old, bf16[16,32,1024]{2,1,0:T(8,128)(2,1)S(1)} %get-tuple-element.9.rows, bf16[3,2,256,256]{3,2,1,0:T(8,128)(2,1)S(1)} %get-tuple-element.10.cols), custom_call_target="tpu_custom_call" | custom-call | tf_op jit(solution)/shard_map/product/pallas_call | solution.py:224
